TPU v7x, 1024 devices: a whole 4x8x16 slice. The times are simulated.
1024 devices in a mesh: outer: 32 (over z, x_lo), inner: 16 (over y, core), chan: 2 (over x_hi).
Axes of the slice: x: 4 (x_hi: 2, x_lo: 2; x = x_hi * 2 + x_lo), y: 8, z: 16, core: 2. Of those that a mesh axis runs over, the one named last changes fastest.
Arguments:
- query_in: bfloat16 [256, 131072], P('chan', ('outer', 'inner')), may hold values from -6 to 6
- key_in: bfloat16 [256, 131072], P('chan', ('outer', 'inner')), may hold values from -6 to 6
- value_in: bfloat16 [256, 131072], P('chan', ('outer', 'inner')), may hold values from -6 to 6
- short_filter: float32 [256, 128], P('chan'), may hold values from -2 to 2
- tap_counts: int32 [16], replicated, may hold values from 1 to 128, as said below
- long_filter: float32 [256, 131072], P('chan', ('outer', 'inner')), may hold values from -0.015625 to 0.015625
- skip_gain: float32 [256], P('chan'), may hold values from -6 to 6
Outputs:
- mixed_out: bfloat16 [256, 131072], P('chan', ('outer', 'inner'))
Inputs may be any that keep to these rules, and one draw needn't show every extreme that they name: tap_counts[g] is how many leading taps channel group g uses; some group uses all 128 taps and some group uses only tap 0.
All inputs are finite; a program needn't handle non-finite values.
Results may differ from a plain program's by a relative error of at most 0.0065.
Values may be sent and summed in bfloat16 or wider, within the bound.
A program may use at most 32 MiB of HBM per device.

v0:
```python
import math

import jax
import jax.numpy as jnp
from jax import lax
from jax.sharding import PartitionSpec as P

GROUP_CH = 16


highest = lax.Precision.HIGHEST


def passed_along(value, axis, steps):
    count = lax.axis_size(axis)
    leading, last = (max(0, -steps), min(count, count - steps))
    return lax.ppermute(value, axis, [(source, source + steps) for source in range(leading, last)])


def for_sending(shard):

    def short(part):
        return part.astype(jnp.bfloat16) if part.dtype == jnp.float32 else part

    return jax.tree.map(short, shard)


def phase_table(first_index, second_index, period, direction_sign):
    product = first_index[:, None] * second_index[None, :] % period
    angles = direction_sign * 2.0 * math.pi / period * product.astype(jnp.float32)
    return (jnp.cos(angles), jnp.sin(angles))


def transform(real_part, imag_part, tables, pattern):
    cos_tab, sin_tab = tables
    out_real = jnp.einsum(pattern, real_part, cos_tab, precision=highest) - jnp.einsum(
        pattern, imag_part, sin_tab, precision=highest
    )
    out_imag = jnp.einsum(pattern, real_part, sin_tab, precision=highest) + jnp.einsum(
        pattern, imag_part, cos_tab, precision=highest
    )
    return (out_real, out_imag)


def rotate(real_part, imag_part, tables):
    cos_tab, sin_tab = tables
    return (real_part * cos_tab - imag_part * sin_tab, real_part * sin_tab + imag_part * cos_tab)


def steps_of(count):
    return jnp.arange(count, dtype=jnp.int32)


def frequency_order(outer_count):
    span_len = 2 * outer_count
    places = steps_of(span_len)
    halves = places // 2
    ordered = jnp.where(places % 2 == 0, halves, (span_len - halves) % span_len)
    return jnp.where(places == 1, outer_count, ordered)


def shards(query_in, key_in, value_in, short_filter, tap_counts, long_filter, skip_gain):
    channels, length = value_in.shape
    tap_len = short_filter.shape[1]
    edge_rows = passed_along(value_in[:, length - tap_len + 1 :], ("outer", "inner"), 1)
    window = jnp.concatenate([edge_rows, value_in], axis=1).astype(jnp.float32)
    chan_ids = lax.axis_index("chan") * channels + steps_of(channels)
    member = chan_ids[:, None] // GROUP_CH == steps_of(tap_counts.shape[0])[None, :]
    counts = jnp.sum(jnp.where(member, tap_counts[None, :], 0), axis=1)
    live_taps = steps_of(tap_len)[None, :] < counts[:, None]
    kernel = jnp.where(live_taps, short_filter, jnp.zeros_like(short_filter))[:, ::-1]
    short_out = lax.conv_general_dilated(
        window[None],
        kernel[:, None, :],
        (1,),
        "VALID",
        dimension_numbers=("NCH", "OIH", "NCH"),
        feature_group_count=channels,
        precision=highest,
    )[0]
    gated_in = key_in.astype(jnp.float32) * short_out
    outer_count = lax.axis_size("outer")
    inner_count = lax.axis_size("inner")
    span_len = 2 * outer_count
    block_len = inner_count * length
    total_len = span_len * block_len
    inner_pos = lax.axis_index("inner")
    g_order = frequency_order(outer_count)
    local_freq = span_len // inner_count
    g_local = lax.dynamic_slice_in_dim(g_order, inner_pos * local_freq, local_freq)
    paired = jnp.stack([gated_in, long_filter]).reshape(2, channels, 1, length)
    regrouped = lax.all_to_all(paired, "outer", split_axis=1, concat_axis=2, tiled=True)
    coarse = phase_table(steps_of(outer_count), g_order, span_len, -1.0)
    token_pos = inner_pos * length + steps_of(length)
    spread_tab = phase_table(g_order, token_pos, total_len, -1.0)
    digit_tab = phase_table(steps_of(inner_count), steps_of(inner_count), inner_count, -1.0)
    fine_rot = phase_table(steps_of(inner_count), steps_of(length), block_len, -1.0)
    last_tab = phase_table(steps_of(length), steps_of(length), length, -1.0)
    spec_real = jnp.einsum("pcar,ag->pcgr", regrouped, coarse[0], precision=highest)
    spec_imag = jnp.einsum("pcar,ag->pcgr", regrouped, coarse[1], precision=highest)
    spec_real, spec_imag = rotate(spec_real, spec_imag, spread_tab)
    stacked = jnp.stack([spec_real, spec_imag])[:, :, :, :, None, :]
    digits = lax.all_to_all(
        for_sending(stacked), "inner", split_axis=3, concat_axis=4, tiled=True
    ).astype(stacked.dtype)
    spec_real, spec_imag = transform(digits[0], digits[1], digit_tab, "pcgir,ij->pcgjr")
    spec_real, spec_imag = rotate(spec_real, spec_imag, fine_rot)
    spec_real, spec_imag = transform(spec_real, spec_imag, last_tab, "pcgjr,rd->pcgjd")
    prod_real = spec_real[0] * spec_real[1] - spec_imag[0] * spec_imag[1]
    prod_imag = spec_real[0] * spec_imag[1] + spec_imag[0] * spec_real[1]
    back_real, back_imag = transform(
        prod_real,
        prod_imag,
        phase_table(steps_of(length), steps_of(length), length, 1.0),
        "cgjd,dr->cgjr",
    )
    back_real, back_imag = rotate(
        back_real, back_imag, phase_table(steps_of(inner_count), steps_of(length), block_len, 1.0)
    )
    back_real, back_imag = transform(
        back_real,
        back_imag,
        phase_table(steps_of(inner_count), steps_of(inner_count), inner_count, 1.0),
        "cgjr,ji->cgir",
    )
    twiddle_tab = phase_table(g_local, steps_of(block_len), total_len, 1.0)
    twiddle_tab = (
        twiddle_tab[0].reshape(local_freq, inner_count, length),
        twiddle_tab[1].reshape(local_freq, inner_count, length),
    )
    back_real, back_imag = rotate(back_real, back_imag, twiddle_tab)
    fine_tab = phase_table(g_local, steps_of(outer_count), span_len, 1.0)
    partial_value = jnp.einsum(
        "cgir,ga->cair", back_real, fine_tab[0], precision=highest
    ) - jnp.einsum("cgir,ga->cair", back_imag, fine_tab[1], precision=highest)
    signal = lax.psum_scatter(partial_value, "inner", scatter_dimension=2, tiled=True)[:, :, 0, :]
    signal = signal / float(total_len)
    returned = lax.all_to_all(signal, "outer", split_axis=1, concat_axis=0, tiled=True).reshape(
        channels, length
    )
    mixed_out = query_in.astype(jnp.float32) * (returned + skip_gain[:, None] * gated_in)
    return mixed_out.astype(jnp.bfloat16)


def solution(mesh):
    placed = (
        P("chan", ("outer", "inner")),
        P("chan", ("outer", "inner")),
        P("chan", ("outer", "inner")),
        P("chan", None),
        P(),
        P("chan", ("outer", "inner")),
        P("chan"),
    )
    return jax.shard_map(
        shards, mesh=mesh, in_specs=placed, out_specs=P("chan", ("outer", "inner")), check_vma=False
    )
```

profile of v0, /device:TPU:1, one launch (start us, length us, event | category | flops | bytes accessed | tf_op | source)
XLA Modules:
  0.0 266.0 jit_solution(5624837726787328134)
XLA Ops:
  6.5 0.8 slice.27
  7.4 4.6 %collective-permute-start = (bf16[128,127]{1,0:T(8,128)(2,1)S(1)}, bf16[128,127]{1,0:T(8,128)(2,1)S(1)}, u32[]{:S(2)}, u32[]{:S(2)}) collective-permute-start(bf16[128,127]{1,0:T(8,128)(2,1)S(1)} %slice.27), channel_id=1, source_target_pairs={{0,2},{2,4},{4,6},{6,8},{8,10},{10,12},{12,14},{14,16},{16,18},{18... | collective-permute-start | bytes 97544 | tf_op jit(solution)/shard_map/ppermute | solution.py:17
  12.0 0.7 select_reduce_fusion
  12.7 0.9 fusion.66
  13.8 1.0 copy.62
  14.8 1.0 copy.65
  15.8 7.7 %collective-permute-done = bf16[128,127]{1,0:T(8,128)(2,1)S(1)} collective-permute-done((bf16[128,127]{1,0:T(8,128)(2,1)S(1)}, bf16[128,127]{1,0:T(8,128)(2,1)S(1)}, u32[]{:S(2)}, u32[]{:S(2)}) %collective-permute-start) | collective-permute-done | bytes 32544 | tf_op jit(solution)/shard_map/ppermute | solution.py:17
  23.5 0.9 maximum_bitcast_fusion.1
  24.6 1.9 fusion.211
  26.6 0.8 copy.66
  27.4 12.2 %all-to-all-start = ((f32[2,128,1,256]{3,0,2,1:T(2,128)}), f32[2,128,1,256]{3,0,2,1:T(2,128)S(1)}, u32[]{:S(2)}, u32[]{:S(2)}) async-start(f32[2,128,1,256]{3,0,2,1:T(2,128)} %copy.66), calls=%async_computation | async-start | bytes 524288 | tf_op jit(solution)/shard_map/all_to_all | solution.py:92
  39.9 18.7 %all-to-all-done = f32[2,128,1,256]{3,0,2,1:T(2,128)S(1)} async-done(((f32[2,128,1,256]{3,0,2,1:T(2,128)}), f32[2,128,1,256]{3,0,2,1:T(2,128)S(1)}, u32[]{:S(2)}, u32[]{:S(2)}) %all-to-all-start) | async-done | bytes 262176 | tf_op jit(solution)/shard_map/all_to_all | solution.py:92
  59.4 0.8 fusion.10
  60.2 1.2 copy.68
  61.4 9.9 %all-to-all-start.1 = ((bf16[2,2,4,64,1,256]{5,2,1,4,0,3:T(4,128)(2,1)}), bf16[2,2,4,64,1,256]{5,2,1,4,0,3:T(4,128)(2,1)S(1)}, u32[]{:S(2)}, u32[]{:S(2)}) async-start(bf16[2,2,4,64,1,256]{5,2,1,4,0,3:T(4,128)(2,1)} %copy.68), calls=%async_computation.1 | async-start | bytes 1048576 | tf_op jit(solution)/shard_map/all_to_all | solution.py:103
  72.2 16.4 %all-to-all-done.1 = bf16[2,2,4,64,1,256]{5,2,1,4,0,3:T(4,128)(2,1)S(1)} async-done(((bf16[2,2,4,64,1,256]{5,2,1,4,0,3:T(4,128)(2,1)}), bf16[2,2,4,64,1,256]{5,2,1,4,0,3:T(4,128)(2,1)S(1)}, u32[]{:S(2)}, u32[]{:S(2)}) %all-to-all-start.1) | async-done | bytes 524320 | tf_op jit(solution)/shard_map/all_to_all | solution.py:103
  90.5 1.6 fusion.6
  92.1 1.6 fusion.4
  93.7 1.6 convolution_subtract_fusion.1
  95.3 1.6 convolution_add_fusion.1
  97.0 1.3 fusion.13
  98.3 1.4 fusion.15
  99.7 1.6 convolution_subtract_fusion.3
  101.3 1.4 convolution_add_fusion.3
  104.4 2.0 fusion.31
  106.4 3.3 %subtract_bitcast_fusion = f32[4,32,16,256]{3,1,2,0:T(8,128)} fusion(f32[32,4,16,256]{3,0,2,1:T(8,128)S(1)} %fusion.31, f32[4,4,16,256]{3,2,1,0:T(8,128)S(1)} %get-tuple-element.9, s32[4]{0:T(128)S(1)} %dynamic_slice.3), kind=kOutput, calls=%fused_computation | convolution fusion | flops 25691904 | bytes 4456464 | tf_op jit(solution)/shard_map/cgir,ga->cair/dot_general | solution.py:135
  109.7 1.3 dynamic-slice
  111.0 117.2 %all-reduce.3.cloned.1.call-done = f32[4,32,16,256]{3,1,2,0:T(8,128)} async-done(((f32[4,32,16,256]{3,1,2,0:T(8,128)}), f32[4,32,16,256]{3,1,2,0:T(8,128)}) %all-reduce.3.cloned.1.call-update) | async-done | bytes 2097168
  228.2 1.6 fusion.40
  230.5 13.8 %all-to-all-start.2 = ((f32[4,32,256]{2,0,1:T(4,128)}), f32[4,32,256]{2,0,1:T(4,128)S(1)}, u32[]{:S(2)}, u32[]{:S(2)}) async-start(f32[4,32,256]{2,0,1:T(4,128)} %copy.73), calls=%async_computation.2 | async-start | bytes 262144 | tf_op jit(solution)/shard_map/all_to_all | solution.py:138
  244.4 13.8 %all-to-all-done.2 = f32[4,32,256]{2,0,1:T(4,128)S(1)} async-done(((f32[4,32,256]{2,0,1:T(4,128)}), f32[4,32,256]{2,0,1:T(4,128)S(1)}, u32[]{:S(2)}, u32[]{:S(2)}) %all-to-all-start.2) | async-done | bytes 131104 | tf_op jit(solution)/shard_map/all_to_all | solution.py:138
  258.4 0.7 copy.75
  (37 shorter events, 7.1 us)
Async XLA Ops:
  7.4 16.1 %collective-permute-start = (bf16[128,127]{1,0:T(8,128)(2,1)S(1)}, bf16[128,127]{1,0:T(8,128)(2,1)S(1)}, u32[]{:S(2)}, u32[]{:S(2)}) collective-permute-start(bf16[128,127]{1,0:T(8,128)(2,1)S(1)} %slice.27), channel_id=1, source_target_pairs={{0,2},{2,4},{4,6},{6,8},{8,10},{10,12},{12,14},{14,16},{16,18},{18... | collective-permute-start | bytes 97544 | tf_op jit(solution)/shard_map/ppermute | solution.py:17
  27.4 31.3 %all-to-all-start = ((f32[2,128,1,256]{3,0,2,1:T(2,128)}), f32[2,128,1,256]{3,0,2,1:T(2,128)S(1)}, u32[]{:S(2)}, u32[]{:S(2)}) async-start(f32[2,128,1,256]{3,0,2,1:T(2,128)} %copy.66), calls=%async_computation | async-start | bytes 524288 | tf_op jit(solution)/shard_map/all_to_all | solution.py:92
  61.4 27.1 %all-to-all-start.1 = ((bf16[2,2,4,64,1,256]{5,2,1,4,0,3:T(4,128)(2,1)}), bf16[2,2,4,64,1,256]{5,2,1,4,0,3:T(4,128)(2,1)S(1)}, u32[]{:S(2)}, u32[]{:S(2)}) async-start(bf16[2,2,4,64,1,256]{5,2,1,4,0,3:T(4,128)(2,1)} %copy.68), calls=%async_computation.1 | async-start | bytes 1048576 | tf_op jit(solution)/shard_map/all_to_all | solution.py:103
  71.4 156.8 %all-reduce.3.cloned.1.call-start = ((), (), s32[]{:S(2)}) async-start(), calls=%async_computation.3 | async-start | bytes 4194304
  109.6 134.6 %copy-start = (bf16[128,256]{1,0:T(8,128)(2,1)S(1)}, bf16[128,256]{1,0:T(8,128)(2,1)}, u32[]{:S(2)}) copy-start(bf16[128,256]{1,0:T(8,128)(2,1)} %param.7) | copy-start | bytes 196612
  109.6 148.7 %copy-start.1 = (f32[128]{0:T(128)S(1)}, f32[128]{0:T(128)}, u32[]{:S(2)}) copy-start(f32[128]{0:T(128)} %param.13) | copy-start | bytes 1540
  230.5 27.7 %all-to-all-start.2 = ((f32[4,32,256]{2,0,1:T(4,128)}), f32[4,32,256]{2,0,1:T(4,128)S(1)}, u32[]{:S(2)}, u32[]{:S(2)}) async-start(f32[4,32,256]{2,0,1:T(4,128)} %copy.73), calls=%async_computation.2 | async-start | bytes 262144 | tf_op jit(solution)/shard_map/all_to_all | solution.py:138
Sparse Core Ops, SparseCore 0:
  109.8 118.3 all-reduce.2
where the time goes:
time: 269 us; the launch traced here: 266 us
  waiting for transfers between devices  174 us (65%)
  starting transfers between devices  40.6 us (15%)
  matrix products  24 us (9%)
  between operations  13.8 us (5%)
  local copies, waits for them, and re-layouts  8.56 us (3%)
  other arithmetic  5.26 us (2%)
    unnamed x2, waiting for transfers between devices  117 us
    all_to_all x1, waiting for transfers between devices, shards(): lax.all_to_all(paired, 'outer', split_axis=1, concat_axis=2, tiled=True)  18.7 us
    all_to_all x1, waiting for transfers between devices, shards(): lax.all_to_all(for_sending(stacked), 'inner', split_axis=3, concat_axis=4...  16.4 us
    all_to_all x1, waiting for transfers between devices, shards(): lax.all_to_all(signal, 'outer', split_axis=1, concat_axis=0, tiled=True)  13.8 us
    all_to_all x1, starting transfers between devices, shards(): lax.all_to_all(signal, 'outer', split_axis=1, concat_axis=0, tiled=True)  13.8 us
    all_to_all x1, starting transfers between devices, shards(): lax.all_to_all(paired, 'outer', split_axis=1, concat_axis=2, tiled=True)  12.2 us
    all_to_all x1, starting transfers between devices, shards(): lax.all_to_all(for_sending(stacked), 'inner', split_axis=3, concat_axis=4...  9.94 us
    ppermute x1, waiting for transfers between devices, passed_along(): lax.ppermute(value, axis, [(source, source + steps) for source in range(l...  7.66 us
  transfers between devices with their start and end apart: 5, of which 5 were waited for; matrix products, arithmetic and copies ran while one was open for 2% of the time, Pallas kernels for 0%

commit v1 on v0

v1 whole, which is shorter than its diff:
```python
import functools
import math

import jax
import jax.numpy as jnp
import numpy as np
from jax import lax
from jax.experimental import pallas as pl
from jax.experimental.pallas import tpu as pltpu
from jax.sharding import PartitionSpec as P

GROUP_CH = 16
LANES = 128
CHANNELS = 128
LENGTH = 256
ROWS = 256
MESH = pl.DeviceIdType.MESH
f32 = jnp.float32
bf16 = jnp.bfloat16


def split_np(table):
    high = table.astype(bf16)
    low = (table - high.astype(np.float64)).astype(bf16)
    return high, low


def fine_tables(outer_count, inner_count):
    set_ch = CHANNELS // outer_count
    local = outer_count // inner_count
    fine = 2 * inner_count
    pos = np.arange(fine).reshape(inner_count, 2)
    freq = np.arange(fine)
    angle = 2.0 * np.pi / fine * (freq[:, None, None] * pos[None] % fine)
    cos, sin = np.cos(angle), np.sin(angle)
    table = np.zeros((2, fine, local, set_ch, inner_count, local, 2, set_ch, 2))
    for one in range(local):
        for chan in range(set_ch):
            table[0, :, one, chan, :, one, 0, chan, :] = cos
            table[0, :, one, chan, :, one, 1, chan, :] = sin
            table[1, :, one, chan, :, one, 0, chan, :] = -sin
            table[1, :, one, chan, :, one, 1, chan, :] = cos
    fine_tab = table.reshape(2 * ROWS, 2 * ROWS)
    steps = np.arange(LANES)
    angle = 2.0 * np.pi / LANES * (steps[:, None] * steps[None] % LANES)
    cos, sin = np.cos(angle), np.sin(angle)
    lane_tab = np.block([[cos, -sin], [sin, cos]])
    fine_all = np.stack([*split_np(fine_tab), *split_np(fine_tab.T)])
    lane_all = np.stack([*split_np(lane_tab), *split_np(lane_tab.T)])
    return fine_all, lane_all


def cos_turns(steps, period):
    half = period // 2
    centred = ((steps + half) & (period - 1)) - half
    x = centred.astype(f32) * (math.pi / period)
    y = x * x
    tail = y * (-1.0 / 5040 + y * (1.0 / 362880 - y * (1.0 / 39916800)))
    s = x * (1.0 + y * (-1.0 / 6 + y * (1.0 / 120 + tail)))
    return 1.0 - 2.0 * s * s


def split(value):
    high = value.astype(bf16)
    return high, (value - high.astype(f32)).astype(bf16)


def dot(left, right):
    return jnp.dot(left, right, preferred_element_type=f32)


def iota2(shape, dim):
    return lax.broadcasted_iota(jnp.int32, shape, dim)


def kernel(
    sizes, query_hbm, key_hbm, value_hbm, taps_hbm, filter_hbm, fine_hbm, lane_hbm, counts_ref, skip_ref,
    out_ref,
    query_ref, key_ref, value_ref, taps_ref, filter_ref, fine_ref, lane_ref,
    edge_ref, window_ref, kept_ref, coarse_ref, back_ref,
    send_h, send_g, send_y, recv_h, recv_g, recv_y,
    mid_send_h, mid_send_g, mid_send_y, mid_recv_h, mid_recv_g, mid_recv_y,
    load_sem, send_sem, recv_sem,
):
    outer_count, inner_count = sizes
    set_ch = CHANNELS // outer_count
    rows = 2 * set_ch
    local = outer_count // inner_count
    fine = 2 * inner_count
    total = outer_count * inner_count * LENGTH
    outer_pos, inner_pos = lax.axis_index("outer"), lax.axis_index("inner")
    block_pos = outer_pos * inner_count + inner_pos
    blocks = outer_count * inner_count

    def block_id(pos):
        return {"outer": pos // inner_count, "inner": lax.rem(pos, inner_count)}

    following = block_id(lax.rem(block_pos + 1, blocks))
    preceding = block_id(lax.rem(block_pos + blocks - 1, blocks))

    def far_first(step, count):
        offset = count // 2 + (1 - 2 * lax.rem(step, 2)) * ((step + 1) // 2)
        return offset

    def outer_peer(step):
        return lax.rem(outer_pos + far_first(step, outer_count), outer_count)

    def inner_peer(step):
        return lax.rem(inner_pos + far_first(step, inner_count), inner_count)

    barrier = pltpu.get_barrier_semaphore()

    def greet_outer(step, carry):
        pl.semaphore_signal(barrier, inc=1, device_id={"outer": outer_peer(step)}, device_id_type=MESH)
        return carry

    def greet_inner(step, carry):
        pl.semaphore_signal(barrier, inc=1, device_id={"inner": inner_peer(step)}, device_id_type=MESH)
        return carry

    lax.fori_loop(0, outer_count - 1, greet_outer, 0)
    lax.fori_loop(0, inner_count - 1, greet_inner, 0)
    pl.semaphore_signal(barrier, inc=1, device_id=following, device_id_type=MESH)
    pl.semaphore_signal(barrier, inc=1, device_id=preceding, device_id_type=MESH)

    loads = [
        pltpu.make_async_copy(source, target, load_sem.at[place])
        for place, (source, target) in enumerate(
            [
                (value_hbm, value_ref), (taps_hbm, taps_ref), (filter_hbm, filter_ref),
                (key_hbm, key_ref), (query_hbm, query_ref), (fine_hbm, fine_ref), (lane_hbm, lane_ref),
            ]
        )
    ]
    for load in loads:
        load.start()

    row = iota2((ROWS, ROWS), 0)
    col = iota2((ROWS, ROWS), 1)
    spread = jnp.where(col == (row & 1) * LANES + (row >> 1), 1.0, 0.0).astype(bf16)

    def to_sets(value):
        halves = jnp.concatenate([value[:, :LANES], value[:, LANES:]], axis=0).astype(bf16)
        return dot(spread, halves).reshape(outer_count, rows, LANES).astype(bf16)

    def from_sets(ref):
        return ref[...].astype(f32).reshape(ROWS, LANES).astype(bf16)

    def exchange_outer(send_ref, recv_ref, place):
        def one(step, carry):
            peer = outer_peer(step)
            pltpu.make_async_remote_copy(
                src_ref=send_ref.at[peer], dst_ref=recv_ref.at[outer_pos],
                send_sem=send_sem.at[place], recv_sem=recv_sem.at[place],
                device_id={"outer": peer}, device_id_type=MESH,
            ).start()
            return carry

        lax.fori_loop(0, outer_count - 1, one, 0)
        pltpu.make_async_copy(send_ref.at[outer_pos], recv_ref.at[outer_pos], recv_sem.at[place]).start()

    def exchange_inner(send_ref, recv_ref, place):
        def one(step, carry):
            peer = inner_peer(step)
            pltpu.make_async_remote_copy(
                src_ref=send_ref.at[peer], dst_ref=recv_ref.at[inner_pos],
                send_sem=send_sem.at[place], recv_sem=recv_sem.at[place],
                device_id={"inner": peer}, device_id_type=MESH,
            ).start()
            return carry

        lax.fori_loop(0, inner_count - 1, one, 0)
        pltpu.make_async_copy(send_ref.at[inner_pos], recv_ref.at[inner_pos], recv_sem.at[place]).start()

    def arrived(recv_ref, place):
        pltpu.make_async_copy(recv_ref, recv_ref, recv_sem.at[place]).wait()

    def sent(send_ref, place):
        part = send_ref.at[pl.ds(0, send_ref.shape[0] - 1)]
        pltpu.make_async_copy(part, part, send_sem.at[place]).wait()

    loads[1].wait()
    lane = iota2((1, LANES), 1)
    counts = jnp.zeros((1, LANES), jnp.int32)
    first_group = lax.axis_index("chan") * (CHANNELS // GROUP_CH)
    for group in range(CHANNELS // GROUP_CH):
        counts = jnp.where(lane // GROUP_CH == group, counts_ref[first_group + group], counts)
    live = iota2((LANES, CHANNELS), 0) < counts
    kept_ref[...] = jnp.where(live, jnp.transpose(taps_ref[...]), 0.0)

    def short_filter(start):
        def eight(step, acc):
            for one in range(8):
                tap = step * 8 + one
                acc = acc + kept_ref[pl.ds(tap, 1), :] * window_ref[pl.ds(start + LANES - tap, LANES), :]
            return acc

        return lax.fori_loop(0, LANES // 8, eight, jnp.zeros((LANES, CHANNELS), f32))

    loads[0].wait()
    window_ref[LANES:, :] = jnp.transpose(value_ref[...].astype(f32))
    short_late = jnp.transpose(short_filter(LANES))

    loads[2].wait()
    send_h[...] = to_sets(filter_ref[...])

    period = 4 * outer_count * fine

    def coarse_table(freq_dim):
        shape = (2 * ROWS, ROWS) if freq_dim == 0 else (ROWS, 2 * ROWS)
        place = iota2(shape, freq_dim)
        token = iota2(shape, 1 - freq_dim)
        freq = place // (2 * rows)
        imag = (place // rows) & 1
        step = (token // rows) * fine + 2 * inner_pos + (token & 1)
        value = cos_turns((4 * freq + 1) * step + imag * (period // 4), period)
        return jnp.where((place & (rows - 1)) == (token & (rows - 1)), value, 0.0)

    coarse_ref[0], coarse_ref[1] = split(coarse_table(0))

    pl.semaphore_wait(barrier, outer_count + inner_count)
    edge = pltpu.make_async_remote_copy(
        src_ref=value_ref.at[:, pl.ds(LANES, LANES)], dst_ref=edge_ref,
        send_sem=send_sem.at[6], recv_sem=recv_sem.at[6],
        device_id=following, device_id_type=MESH,
    )
    edge.start()
    exchange_outer(send_h, recv_h, 0)

    loads[3].wait()
    edge.wait_recv()
    before = jnp.transpose(edge_ref[...].astype(f32))
    window_ref[:LANES, :] = jnp.where(block_pos == 0, jnp.zeros_like(before), before)
    short_early = jnp.transpose(short_filter(0))
    gated = key_ref[...].astype(f32) * jnp.concatenate([short_early, short_late], axis=1)
    send_g[...] = to_sets(gated)
    exchange_outer(send_g, recv_g, 1)

    back_ref[0], back_ref[1] = split(coarse_table(1))
    place = iota2((ROWS, LANES), 0)
    near = iota2((ROWS, LANES), 1)
    freq = inner_pos * local + ((place // set_ch) & (local - 1))
    turn = (4 * freq + 1 + 4 * outer_count * (place // (set_ch * local))) * near
    twist_cos = cos_turns(turn, 4 * total)
    twist_sin = cos_turns(turn + 3 * total, 4 * total)
    skip_eye = iota2((CHANNELS, CHANNELS), 0) == iota2((CHANNELS, CHANNELS), 1)
    skip_col = jnp.sum(jnp.where(skip_eye, skip_ref[...], 0.0), axis=1, keepdims=True)
    skipped = skip_col * gated
    loads[4].wait()
    loads[5].wait()
    loads[6].wait()

    def coarse_forward(recv_ref, send_ref):
        block = from_sets(recv_ref)
        value = dot(coarse_ref[0], block) + dot(coarse_ref[1], block)
        send_ref[...] = value.astype(bf16).reshape(inner_count, 2 * local * rows, LANES)

    def fine_forward(recv_ref):
        block = recv_ref[...].reshape(2 * ROWS, LANES)
        value = dot(fine_ref[0], block) + dot(fine_ref[1], block)
        real, imag = value[:ROWS], value[ROWS:]
        turned = jnp.concatenate(
            [real * twist_cos + imag * twist_sin, imag * twist_cos - real * twist_sin], axis=1
        )
        high, low = split(turned)
        return dot(high, lane_ref[0]) + dot(low, lane_ref[0]) + dot(high, lane_ref[1])

    arrived(recv_h, 0)
    coarse_forward(recv_h, mid_send_h)
    exchange_inner(mid_send_h, mid_recv_h, 2)
    arrived(recv_g, 1)
    coarse_forward(recv_g, mid_send_g)
    exchange_inner(mid_send_g, mid_recv_g, 3)

    arrived(mid_recv_h, 2)
    spec_h = fine_forward(mid_recv_h) * (1.0 / total)
    arrived(mid_recv_g, 3)
    spec_g = fine_forward(mid_recv_g)

    h_real, h_imag = spec_h[:, :LANES], spec_h[:, LANES:]
    g_real, g_imag = spec_g[:, :LANES], spec_g[:, LANES:]
    product = jnp.concatenate(
        [g_real * h_real - g_imag * h_imag, g_real * h_imag + g_imag * h_real], axis=1
    )
    high, low = split(product)
    value = dot(high, lane_ref[2]) + dot(low, lane_ref[2]) + dot(high, lane_ref[3])
    real, imag = value[:, :LANES], value[:, LANES:]
    turned = jnp.concatenate(
        [real * twist_cos - imag * twist_sin, imag * twist_cos + real * twist_sin], axis=0
    )
    high, low = split(turned)
    value = dot(fine_ref[2], high) + dot(fine_ref[2], low) + dot(fine_ref[3], high)
    mid_send_y[...] = value.astype(bf16).reshape(inner_count, 2 * local * rows, LANES)
    exchange_inner(mid_send_y, mid_recv_y, 4)

    gather = jnp.where(row == (col & 1) * LANES + (col >> 1), 1.0, 0.0).astype(bf16)
    arrived(mid_recv_y, 4)
    block = mid_recv_y[...].reshape(2 * ROWS, LANES)
    value = dot(back_ref[0], block) + dot(back_ref[1], block)
    send_y[...] = value.reshape(outer_count, rows, LANES).astype(bf16)
    exchange_outer(send_y, recv_y, 5)

    arrived(recv_y, 5)
    halves = dot(gather, from_sets(recv_y))
    long_out = jnp.concatenate([halves[:LANES], halves[LANES:]], axis=1)
    out_ref[...] = (query_ref[...].astype(f32) * (long_out + skipped)).astype(bf16)

    edge.wait_send()
    for place, send_ref in enumerate([send_h, send_g, mid_send_h, mid_send_g, mid_send_y, send_y]):
        sent(send_ref, place)


def shards(sizes, query_in, key_in, value_in, short_filter, tap_counts, long_filter, skip_gain):
    outer_count, inner_count = sizes
    fine_all, lane_all = fine_tables(outer_count, inner_count)
    coarse_rows = 2 * CHANNELS // outer_count
    far = pltpu.VMEM((outer_count, coarse_rows, LANES), bf16)
    mid = pltpu.VMEM((inner_count, 2 * ROWS // inner_count, LANES), bf16)
    anywhere = pl.BlockSpec(memory_space=pl.ANY)
    return pl.pallas_call(
        functools.partial(kernel, sizes),
        out_shape=jax.ShapeDtypeStruct((CHANNELS, LENGTH), bf16),
        in_specs=[anywhere] * 7
        + [pl.BlockSpec(memory_space=pltpu.SMEM), pl.BlockSpec(memory_space=pltpu.VMEM)],
        out_specs=pl.BlockSpec(memory_space=pltpu.VMEM),
        scratch_shapes=[
            pltpu.VMEM((CHANNELS, LENGTH), bf16),
            pltpu.VMEM((CHANNELS, LENGTH), bf16),
            pltpu.VMEM((CHANNELS, LENGTH), bf16),
            pltpu.VMEM((CHANNELS, LANES), f32),
            pltpu.VMEM((CHANNELS, LENGTH), f32),
            pltpu.VMEM(fine_all.shape, bf16),
            pltpu.VMEM(lane_all.shape, bf16),
            pltpu.VMEM((CHANNELS, LANES), bf16),
            pltpu.VMEM((LANES + LENGTH, CHANNELS), f32),
            pltpu.VMEM((LANES, CHANNELS), f32),
            pltpu.VMEM((2, 2 * ROWS, ROWS), bf16),
            pltpu.VMEM((2, ROWS, 2 * ROWS), bf16),
            *[far] * 6,
            *[mid] * 6,
            pltpu.SemaphoreType.DMA((7,)),
            pltpu.SemaphoreType.DMA((7,)),
            pltpu.SemaphoreType.DMA((7,)),
        ],
        compiler_params=pltpu.CompilerParams(collective_id=0, has_side_effects=True),
    )(
        query_in, key_in, value_in, short_filter, long_filter,
        jnp.asarray(fine_all), jnp.asarray(lane_all), tap_counts, skip_gain.reshape(1, CHANNELS),
    )


def solution(mesh):
    placed = (
        P("chan", ("outer", "inner")),
        P("chan", ("outer", "inner")),
        P("chan", ("outer", "inner")),
        P("chan", None),
        P(),
        P("chan", ("outer", "inner")),
        P("chan"),
    )
    sizes = (mesh.shape["outer"], mesh.shape["inner"])
    return jax.shard_map(
        functools.partial(shards, sizes),
        mesh=mesh,
        in_specs=placed,
        out_specs=P("chan", ("outer", "inner")),
        check_vma=False,
    )
```

time: 269 us -> 58.3 us (0.22); the launches traced: 266 us -> 58.1 us
  waiting for transfers between devices: 174 us -> 0 us
  Pallas kernels: 0 us -> 56.6 us
  starting transfers between devices: 40.6 us -> 0 us
  matrix products: 24 us -> 0 us
  between operations: 13.8 us -> 0.01 us
  local copies, waits for them, and re-layouts: 8.56 us -> 1.47 us
  other arithmetic: 5.26 us -> 0 us
    unnamed x2 -> x0, waiting for transfers between devices: 117 us -> none
    pallas_call x0 -> x1, Pallas kernels: none -> 56.6 us  [shards(): pl.pallas_call(functools.partial(kernel, sizes), out_shape=jax.ShapeDtype...]
    all_to_all x3 -> x0, waiting for transfers between devices: 49 us -> none  [the longest x1 18.7 us: shards(): lax.all_to_all(paired, 'outer', split_axis=1, concat_axis=2, tiled=True)]
    all_to_all x3 -> x0, starting transfers between devices: 35.8 us -> none  [the longest x1 13.8 us: shards(): lax.all_to_all(signal, 'outer', split_axis=1, concat_axis=0, tiled=True)]
    dot_general x20 -> x0, matrix products: 22 us -> none  [the longest x4 3.98 us: transform(): jnp.einsum(pattern, imag_part, sin_tab, precision=highest)]
    ppermute x1 -> x0, waiting for transfers between devices: 7.66 us -> none  [passed_along(): lax.ppermute(value, axis, [(source, source + steps) for source in range(l...]
    ppermute x1 -> x0, starting transfers between devices: 4.57 us -> none  [passed_along(): lax.ppermute(value, axis, [(source, source + steps) for source in range(l...]
  transfers between devices with their start and end apart: 5 -> 0, of which waited for: 5 -> 0; matrix products, arithmetic and copies ran while one was open for 2% -> 0% of each run, Pallas kernels for 0% -> 0%
where the time goes in v1:
time: 58.3 us; the launch traced here: 58.1 us
  Pallas kernels  56.6 us (97%)
  local copies, waits for them, and re-layouts  1.47 us (3%)
    pallas_call x1, Pallas kernels, shards(): pl.pallas_call(functools.partial(kernel, sizes), out_shape=jax.ShapeDtype...  56.6 us
    unnamed x1, local copies, waits for them, and re-layouts  1.47 us

profile of v1, /device:TPU:1, one launch (start us, length us, event | category | flops | bytes accessed | tf_op | source)
XLA Modules:
  0.0 58.1 jit_solution(840927170099332074)
XLA Ops:
  0.0 56.6 %shard_map.91 = bf16[128,256]{1,0:T(8,128)(2,1)} custom-call(bf16[128,256]{1,0:T(8,128)(2,1)} %query_hbm.1, bf16[128,256]{1,0:T(8,128)(2,1)} %key_hbm.1, bf16[128,256]{1,0:T(8,128)(2,1)} %value_hbm.1, f32[128,128]{1,0:T(8,128)} %taps_hbm.1, f32[128,256]{1,0:T(8,128)} %filter_hbm.1, bf16[4,512,512]{2,1,0:T(8,128)(2,1)} %constant.4.clone.fine_hbm, ...), custom_call_target="tpu_custom_call" | custom-call | tf_op jit(solution)/shard_map/pallas_call | solution.py:320
  56.6 1.5 %copy.11 = bf16[128,256]{1,0:T(8,128)(2,1)} copy(bf16[128,256]{1,0:T(8,128)(2,1)} %shard_map.91) | data formatting | bytes 131072

commit v2 on v1

v2 whole, which is shorter than its diff:
```python
import functools
import math

import jax
import jax.numpy as jnp
import numpy as np
from jax import lax
from jax.experimental import pallas as pl
from jax.experimental.pallas import tpu as pltpu
from jax.sharding import PartitionSpec as P

GROUP_CH = 16
LANES = 128
SUB = 8
PAIR = 4
CHANNELS = 128
LENGTH = 256
MESH = pl.DeviceIdType.MESH
f32 = jnp.float32
bf16 = jnp.bfloat16


def lane_tables():
    steps = np.arange(LANES)
    angle = 2.0 * np.pi / LANES * (steps[:, None] * steps[None] % LANES)
    cos, sin = np.cos(angle), np.sin(angle)
    table = np.block([[cos, -sin], [sin, cos]])
    parts = []
    for one in (table, table.T):
        high = one.astype(bf16)
        parts += [high, (one - high.astype(np.float64)).astype(bf16)]
    return np.stack(parts)


def cos_turns(steps, period):
    half = period // 2
    centred = ((steps + half) & (period - 1)) - half
    x = centred.astype(f32) * (math.pi / period)
    y = x * x
    tail = y * (-1.0 / 5040 + y * (1.0 / 362880 - y * (1.0 / 39916800)))
    s = x * (1.0 + y * (-1.0 / 6 + y * (1.0 / 120 + tail)))
    return 1.0 - 2.0 * s * s


def split(value):
    high = value.astype(bf16)
    return high, (value - high.astype(f32)).astype(bf16)


def dot(left, right):
    return jnp.dot(left, right, preferred_element_type=f32)


def iota(shape, dim):
    return lax.broadcasted_iota(jnp.int32, shape, dim)


def turned(value, table, inverse=False):
    real, imag = value
    cos, sin = table
    if inverse:
        return real * cos - imag * sin, imag * cos + real * sin
    return real * cos + imag * sin, imag * cos - real * sin


def four(parts, inverse):
    (ar, ai), (br, bi), (cr, ci), (dr, di) = parts
    sr, si, tr, ti = ar + cr, ai + ci, ar - cr, ai - ci
    ur, ui, vr, vi = br + dr, bi + di, br - dr, bi - di
    one, three = (tr + vi, ti - vr), (tr - vi, ti + vr)
    if inverse:
        one, three = three, one
    return [(sr + ur, si + ui), one, (sr - ur, si - ui), three]


def scalar_turn(count, period):
    return math.cos(2.0 * math.pi * count / period), math.sin(2.0 * math.pi * count / period)


def stacked(parts, axis=0):
    return tuple(jnp.stack([part[which] for part in parts], axis=axis) for which in (0, 1))


def transform32(value, table, inverse):
    parts = four([tuple(x[8 * q : 8 * q + 8] for x in value) for q in range(4)], inverse)
    parts = [parts[0]] + [turned(parts[p], tuple(t[p - 1] for t in table), inverse) for p in (1, 2, 3)]
    value = stacked(parts)
    parts = four([tuple(x[:, 2 * q : 2 * q + 2] for x in value) for q in range(4)], inverse)
    sums, gaps = [], []
    for p, part in enumerate(parts):
        even, odd = tuple(x[:, 0] for x in part), tuple(x[:, 1] for x in part)
        if p == 2:
            odd = (-odd[1], odd[0]) if inverse else (odd[1], -odd[0])
        elif p:
            odd = turned(odd, scalar_turn(p, 8), inverse)
        sums.append(tuple(x + y for x, y in zip(even, odd)))
        gaps.append(tuple(x - y for x, y in zip(even, odd)))
    both = stacked(sums + gaps)
    return tuple(x.reshape((32,) + x.shape[2:]) for x in both)


def paired(first, second):
    low = iota(first.shape, first.ndim - 2) < PAIR
    first_moved = jnp.roll(first, PAIR, axis=first.ndim - 2)
    second_moved = jnp.roll(second, PAIR, axis=second.ndim - 2)
    return jnp.where(low, first, second_moved), jnp.where(low, first_moved, second)


def kernel(
    sizes, query_hbm, key_hbm, value_hbm, taps_hbm, filter_hbm, lane_hbm, counts_ref, skip_ref,
    out_ref,
    query_ref, key_ref, value_ref, taps_ref, filter_ref, lane_ref,
    edge_ref, window_ref, border_ref, kept_ref, skipped_ref, twist_ref, twiddle_ref, small_ref, spec_ref, start_ref,
    send_h, send_g, send_y, recv_h, recv_g, recv_y, mid_send, mid_recv,
    load_sem, far_send, far_recv, mid_send_sem, mid_recv_sem, edge_sem,
):
    outer_count, inner_count = sizes
    blocks = outer_count * inner_count
    total = blocks * LENGTH
    fine = 2 * inner_count
    outer_pos, inner_pos = lax.axis_index("outer"), lax.axis_index("inner")
    block_pos = outer_pos * inner_count + inner_pos

    def block_id(pos):
        return {"outer": pos // inner_count, "inner": lax.rem(pos, inner_count)}

    following = block_id(lax.rem(block_pos + 1, blocks))
    preceding = block_id(lax.rem(block_pos + blocks - 1, blocks))

    def order(count):
        return sorted(range(1, count), key=lambda offset: -min(offset, count - offset))

    loads = [
        pltpu.make_async_copy(source, target, load_sem.at[number])
        for number, (source, target) in enumerate(
            [
                (value_hbm, value_ref), (filter_hbm, filter_ref), (taps_hbm, taps_ref),
                (key_hbm, key_ref), (query_hbm, query_ref), (lane_hbm, lane_ref),
            ]
        )
    ]
    for load in loads:
        load.start()

    barrier = pltpu.get_barrier_semaphore()

    def greet(device):
        pl.semaphore_signal(barrier, inc=1, device_id=device, device_id_type=MESH)

    def greet_inner(step, carry):
        greet({"inner": lax.rem(inner_pos + step, inner_count)})
        return carry

    def greet_outer(step, carry):
        greet({"outer": lax.rem(outer_pos + step, outer_count)})
        return carry

    greet(following)
    greet(preceding)
    lax.fori_loop(1, inner_count, greet_inner, 0)
    lax.fori_loop(1, outer_count, greet_outer, 0)

    def to_sets(value):
        parts = [value[:, LANES * n : LANES * (n + 1)].reshape(outer_count // 2, SUB, LANES) for n in (0, 1)]
        both = jnp.stack(paired(*parts), axis=1)
        return both.reshape(outer_count, SUB, LANES).astype(bf16)

    def arrived(ref, sem):
        pltpu.make_async_copy(ref, ref, sem).wait()

    def sent(ref, count, sem):
        part = ref.at[pl.ds(0, count)]
        pltpu.make_async_copy(part, part, sem).wait()

    def to_outer(send_ref, recv_ref, stream):
        for offset in order(outer_count):
            target = lax.rem(outer_pos + offset, outer_count)
            pltpu.make_async_remote_copy(
                src_ref=send_ref.at[target], dst_ref=recv_ref.at[outer_pos],
                send_sem=far_send.at[stream], recv_sem=far_recv.at[stream],
                device_id={"outer": target}, device_id_type=MESH,
            ).start()
        pltpu.make_async_copy(send_ref.at[outer_pos], recv_ref.at[outer_pos], far_recv.at[stream]).start()

    loads[1].wait()
    send_h[...] = to_sets(filter_ref[...])
    loads[0].wait()
    window_ref[:LANES, :] = jnp.zeros((LANES, CHANNELS), f32)
    window_ref[LANES:, :] = jnp.transpose(value_ref[...].astype(f32))
    border_ref[LANES:, :] = jnp.zeros((LANES, CHANNELS), f32)

    pl.semaphore_wait(barrier, outer_count + inner_count)
    edge = pltpu.make_async_remote_copy(
        src_ref=value_ref.at[:, pl.ds(LANES, LANES)], dst_ref=edge_ref,
        send_sem=edge_sem.at[0], recv_sem=edge_sem.at[1],
        device_id=following, device_id_type=MESH,
    )

    edge.start()
    to_outer(send_h, recv_h, 0)

    loads[2].wait()
    lane = iota((1, LANES), 1)
    counts = jnp.zeros((1, LANES), jnp.int32)
    first_group = lax.axis_index("chan") * (CHANNELS // GROUP_CH)
    for group in range(CHANNELS // GROUP_CH):
        counts = jnp.where(lane // GROUP_CH == group, counts_ref[first_group + group], counts)
    live = iota((LANES, CHANNELS), 0) < counts
    kept_ref[...] = jnp.where(live, jnp.transpose(taps_ref[...]), 0.0)

    def short_filter(source_ref, start, rows, first):
        def eight(step, acc):
            for one in range(8):
                tap = step * 8 + one
                acc = acc + kept_ref[pl.ds(tap, 1), :] * source_ref[pl.ds(start + LANES - tap, rows), :]
            return acc

        return lax.fori_loop(first // 8, LANES // 8, eight, jnp.zeros((rows, CHANNELS), f32))

    own_late = jnp.transpose(short_filter(window_ref, LANES, LANES, 0))
    own_early = short_filter(window_ref, 0, LANES, 0)

    loads[3].wait()

    edge.wait_recv()
    before = jnp.transpose(edge_ref[...].astype(f32))
    border_ref[:LANES, :] = jnp.where(block_pos == 0, jnp.zeros_like(before), before)

    pieces = [short_filter(border_ref, 64 * n, 64, 64 * n) for n in (0, 1)]
    short_early = jnp.transpose(own_early + jnp.concatenate(pieces, axis=0))
    gated = key_ref[...].astype(f32) * jnp.concatenate([short_early, own_late], axis=1)
    send_g[...] = to_sets(gated)
    to_outer(send_g, recv_g, 1)

    skip_eye = iota((CHANNELS, CHANNELS), 0) == iota((CHANNELS, CHANNELS), 1)
    skip_col = jnp.sum(jnp.where(skip_eye, skip_ref[...], 0.0), axis=1, keepdims=True)
    skipped_ref[...] = skip_col * gated
    loads[4].wait()
    loads[5].wait()

    shape = (fine, SUB, LANES)
    lead, near = iota(shape, 0), iota(shape, 2)
    freq = 4 * (2 * inner_pos + iota(shape, 1) // PAIR) + 1
    small_shape = (24, SUB, LANES)
    small_turn = (iota(small_shape, 0) // 8 + 1) * (iota(small_shape, 0) & 7)
    for number, shift in ((0, 0), (1, 3)):
        start_ref[number] = cos_turns(lead + shift * outer_count, 4 * outer_count)
        small_ref[number] = cos_turns(small_turn + shift * 8, 32)
        twist_ref[number] = cos_turns(freq * lead + shift * outer_count * fine, 4 * outer_count * fine)
        twiddle_ref[number] = cos_turns((freq + 4 * outer_count * lead) * near + shift * total, 4 * total)

    def pair(ref):
        return ref[0], ref[1]

    def small():
        return tuple(small_ref[number].reshape(3, 8, SUB, LANES) for number in (0, 1))

    def exchange_inner(stream):
        for offset in order(inner_count):
            peer = lax.rem(inner_pos + offset, inner_count)
            pltpu.make_async_remote_copy(
                src_ref=mid_send.at[stream, peer], dst_ref=mid_recv.at[stream, inner_pos],
                send_sem=mid_send_sem.at[stream], recv_sem=mid_recv_sem.at[stream],
                device_id={"inner": peer}, device_id_type=MESH,
            ).start()
        pltpu.make_async_copy(
            mid_send.at[stream, inner_pos], mid_recv.at[stream, inner_pos], mid_recv_sem.at[stream]
        ).start()

    def mid_message(halves):
        both = jnp.stack([halves[0][0], halves[0][1], halves[1][0], halves[1][1]], axis=1)
        return both.reshape(inner_count, 4 * SUB, LANES).astype(bf16)

    def coarse_forward(recv_ref, stream):
        arrived(recv_ref, far_recv.at[stream])
        value = recv_ref[...].astype(f32)
        value = transform32((value * start_ref[0], -value * start_ref[1]), small(), False)
        parts = [x.reshape(inner_count, 2, SUB, LANES) for x in value]
        real, imag = [paired(x[:, 0], x[:, 1]) for x in parts]
        mid_send[stream] = mid_message([(real[0], imag[0]), (real[1], imag[1])])
        exchange_inner(stream)

    def fine_forward(stream):
        arrived(mid_recv.at[stream], mid_recv_sem.at[stream])
        both = mid_recv[stream].astype(f32).reshape(fine, 2, SUB, LANES)
        value = transform32(turned((both[:, 0], both[:, 1]), pair(twist_ref)), small(), False)
        value = turned(value, pair(twiddle_ref))
        block = jnp.concatenate([x.reshape(fine * SUB, LANES) for x in value], axis=1)
        high, low = split(block)
        return dot(high, lane_ref[0]) + dot(low, lane_ref[0]) + dot(high, lane_ref[1])

    def halves(spec):
        return spec[:, :LANES], spec[:, LANES:]

    coarse_forward(recv_h, 0)
    coarse_forward(recv_g, 1)
    spec_ref[...] = fine_forward(0) * (1.0 / total)
    (ar, ai), (br, bi) = halves(spec_ref[...]), halves(fine_forward(1))
    high, low = split(jnp.concatenate([ar * br - ai * bi, ar * bi + ai * br], axis=1))
    block = dot(high, lane_ref[2]) + dot(low, lane_ref[2]) + dot(high, lane_ref[3])
    value = tuple(x.reshape(fine, SUB, LANES) for x in halves(block))
    value = transform32(turned(value, pair(twiddle_ref), True), small(), True)
    value = tuple(x.reshape(inner_count, 2, SUB, LANES) for x in turned(value, pair(twist_ref), True))
    mid_send[2] = mid_message([(value[0][:, n], value[1][:, n]) for n in (0, 1)])
    exchange_inner(2)

    arrived(mid_recv.at[2], mid_recv_sem.at[2])
    both = mid_recv[2].astype(f32).reshape(inner_count, 2, 2, SUB, LANES)
    parts = [jnp.stack(paired(both[:, 0, n], both[:, 1, n]), axis=1) for n in (0, 1)]
    real, imag = transform32(tuple(x.reshape(outer_count, SUB, LANES) for x in parts), small(), True)
    send_y[...] = (real * start_ref[0] - imag * start_ref[1]).astype(bf16)
    to_outer(send_y, recv_y, 2)

    arrived(recv_y, far_recv.at[2])
    sets = recv_y[...].astype(f32).reshape(outer_count // 2, 2, SUB, LANES)
    for n, long_out in enumerate(paired(sets[:, 0], sets[:, 1])):
        span = pl.ds(LANES * n, LANES)
        long_out = long_out.reshape(CHANNELS, LANES)
        out_ref[:, span] = (query_ref[:, span].astype(f32) * (long_out + skipped_ref[:, span])).astype(bf16)

    edge.wait_send()
    for stream, send_ref in enumerate((send_h, send_g, send_y)):
        sent(send_ref, outer_count - 1, far_send.at[stream])
        sent(mid_send.at[stream], inner_count - 1, mid_send_sem.at[stream])


def shards(sizes, query_in, key_in, value_in, short_filter, tap_counts, long_filter, skip_gain):
    outer_count, inner_count = sizes
    lane_all = lane_tables()
    sets = (outer_count, SUB, LANES)
    fine = (2 * inner_count, SUB, LANES)
    anywhere = pl.BlockSpec(memory_space=pl.ANY)
    return pl.pallas_call(
        functools.partial(kernel, sizes),
        out_shape=jax.ShapeDtypeStruct((CHANNELS, LENGTH), bf16),
        in_specs=[anywhere] * 6
        + [pl.BlockSpec(memory_space=pltpu.SMEM), pl.BlockSpec(memory_space=pltpu.VMEM)],
        out_specs=pl.BlockSpec(memory_space=pltpu.VMEM),
        scratch_shapes=[
            pltpu.VMEM((CHANNELS, LENGTH), bf16),
            pltpu.VMEM((CHANNELS, LENGTH), bf16),
            pltpu.VMEM((CHANNELS, LENGTH), bf16),
            pltpu.VMEM((CHANNELS, LANES), f32),
            pltpu.VMEM((CHANNELS, LENGTH), f32),
            pltpu.VMEM(lane_all.shape, bf16),
            pltpu.VMEM((CHANNELS, LANES), bf16),
            pltpu.VMEM((LANES + LENGTH, CHANNELS), f32),
            pltpu.VMEM((2 * LANES, CHANNELS), f32),
            pltpu.VMEM((LANES, CHANNELS), f32),
            pltpu.VMEM((CHANNELS, LENGTH), f32),
            pltpu.VMEM((2, *fine), f32),
            pltpu.VMEM((2, *fine), f32),
            pltpu.VMEM((2, 24, SUB, LANES), f32),
            pltpu.VMEM((fine[0] * SUB, 2 * LANES), f32),
            pltpu.VMEM((2, *fine), f32),
            *[pltpu.VMEM(sets, bf16)] * 6,
            pltpu.VMEM((3, inner_count, 4 * SUB, LANES), bf16),
            pltpu.VMEM((3, inner_count, 4 * SUB, LANES), bf16),
            pltpu.SemaphoreType.DMA((6,)),
            pltpu.SemaphoreType.DMA((3,)),
            pltpu.SemaphoreType.DMA((3,)),
            pltpu.SemaphoreType.DMA((3,)),
            pltpu.SemaphoreType.DMA((3,)),
            pltpu.SemaphoreType.DMA((2,)),
        ],
        compiler_params=pltpu.CompilerParams(collective_id=0, has_side_effects=True),
    )(
        query_in, key_in, value_in, short_filter, long_filter,
        jnp.asarray(lane_all), tap_counts, skip_gain.reshape(1, CHANNELS),
    )


def solution(mesh):
    placed = (
        P("chan", ("outer", "inner")),
        P("chan", ("outer", "inner")),
        P("chan", ("outer", "inner")),
        P("chan", None),
        P(),
        P("chan", ("outer", "inner")),
        P("chan"),
    )
    sizes = (mesh.shape["outer"], mesh.shape["inner"])
    return jax.shard_map(
        functools.partial(shards, sizes),
        mesh=mesh,
        in_specs=placed,
        out_specs=P("chan", ("outer", "inner")),
        check_vma=False,
    )
```

time: 58.3 us -> 56 us (0.961)
  Pallas kernels: 56.6 us -> 54.3 us
    pallas_call x1, Pallas kernels: 56.6 us -> 54.3 us  [shards(): pl.pallas_call(functools.partial(kernel, sizes), out_shape=jax.ShapeDtype...]
where the time goes in v2:
time: 56 us; the launch traced here: 55.8 us
  Pallas kernels  54.3 us (97%)
  local copies, waits for them, and re-layouts  1.47 us (3%)
    pallas_call x1, Pallas kernels, shards(): pl.pallas_call(functools.partial(kernel, sizes), out_shape=jax.ShapeDtype...  54.3 us
    unnamed x1, local copies, waits for them, and re-layouts  1.47 us

profile of v2, /device:TPU:1, one launch (start us, length us, event | category | flops | bytes accessed | tf_op | source)
XLA Modules:
  0.0 55.8 jit_solution(9212311748168480730)
XLA Ops:
  0.0 54.3 %shard_map.82 = bf16[128,256]{1,0:T(8,128)(2,1)} custom-call(bf16[128,256]{1,0:T(8,128)(2,1)} %query_hbm.1, bf16[128,256]{1,0:T(8,128)(2,1)} %key_hbm.1, bf16[128,256]{1,0:T(8,128)(2,1)} %value_hbm.1, f32[128,128]{1,0:T(8,128)} %taps_hbm.1, f32[128,256]{1,0:T(8,128)} %filter_hbm.1, bf16[4,256,256]{2,1,0:T(8,128)(2,1)} %constant.2.clone.lane_hbm, ...), custom_call_target="tpu_custom_call" | custom-call | tf_op jit(solution)/shard_map/pallas_call | solution.py:333
  54.3 1.5 %copy.10 = bf16[128,256]{1,0:T(8,128)(2,1)} copy(bf16[128,256]{1,0:T(8,128)(2,1)} %shard_map.82) | data formatting | bytes 131072

commit v3 on v2

--- a/solution.py
+++ b/solution.py
@@ -110,7 +110,7 @@
     sizes, query_hbm, key_hbm, value_hbm, taps_hbm, filter_hbm, lane_hbm, counts_ref, skip_ref,
     out_ref,
     query_ref, key_ref, value_ref, taps_ref, filter_ref, lane_ref,
-    edge_ref, window_ref, border_ref, kept_ref, skipped_ref, twist_ref, twiddle_ref, small_ref, spec_ref, start_ref,
+    edge_ref, window_ref, kept_ref, skipped_ref, twist_ref, twiddle_ref, small_ref, spec_ref, start_ref,
     send_h, send_g, send_y, recv_h, recv_g, recv_y, mid_send, mid_recv,
     load_sem, far_send, far_recv, mid_send_sem, mid_recv_sem, edge_sem,
 ):
@@ -147,18 +147,12 @@
     def greet(device):
         pl.semaphore_signal(barrier, inc=1, device_id=device, device_id_type=MESH)
 
-    def greet_inner(step, carry):
-        greet({"inner": lax.rem(inner_pos + step, inner_count)})
-        return carry
-
-    def greet_outer(step, carry):
-        greet({"outer": lax.rem(outer_pos + step, outer_count)})
-        return carry
-
+    for offset in order(outer_count):
+        greet({"outer": lax.rem(outer_pos + offset, outer_count)})
+    for offset in order(inner_count):
+        greet({"inner": lax.rem(inner_pos + offset, inner_count)})
     greet(following)
     greet(preceding)
-    lax.fori_loop(1, inner_count, greet_inner, 0)
-    lax.fori_loop(1, outer_count, greet_outer, 0)
 
     def to_sets(value):
         parts = [value[:, LANES * n : LANES * (n + 1)].reshape(outer_count // 2, SUB, LANES) for n in (0, 1)]
@@ -185,9 +179,7 @@
     loads[1].wait()
     send_h[...] = to_sets(filter_ref[...])
     loads[0].wait()
-    window_ref[:LANES, :] = jnp.zeros((LANES, CHANNELS), f32)
     window_ref[LANES:, :] = jnp.transpose(value_ref[...].astype(f32))
-    border_ref[LANES:, :] = jnp.zeros((LANES, CHANNELS), f32)
 
     pl.semaphore_wait(barrier, outer_count + inner_count)
     edge = pltpu.make_async_remote_copy(
@@ -208,27 +200,50 @@
     live = iota((LANES, CHANNELS), 0) < counts
     kept_ref[...] = jnp.where(live, jnp.transpose(taps_ref[...]), 0.0)
 
-    def short_filter(source_ref, start, rows, first):
-        def eight(step, acc):
-            for one in range(8):
-                tap = step * 8 + one
-                acc = acc + kept_ref[pl.ds(tap, 1), :] * source_ref[pl.ds(start + LANES - tap, rows), :]
-            return acc
-
-        return lax.fori_loop(first // 8, LANES // 8, eight, jnp.zeros((rows, CHANNELS), f32))
-
-    own_late = jnp.transpose(short_filter(window_ref, LANES, LANES, 0))
-    own_early = short_filter(window_ref, 0, LANES, 0)
+    groups = LANES // SUB
+
+    def tap(residue, step):
+        return kept_ref[pl.ds(residue + SUB * step, 1), :]
+
+    def short_late(residue, acc):
+        rows = SUB * (2 * groups - 1)
+        block = window_ref[pl.ds(LANES + SUB - residue, rows), :]
+        for step in range(groups):
+            start = SUB * (groups - 1 - step)
+            acc = acc + tap(residue, step) * block[start : start + LANES]
+        return acc
+
+    def short_early(first, pairs):
+        def one(residue, acc):
+            acc = list(acc)
+            block = window_ref[pl.ds(first - residue, LANES), :]
+            for step in range(groups):
+                weight = tap(residue, step)
+                for place, source in pairs(step):
+                    acc[place] = acc[place] + weight * block[SUB * source : SUB * (source + 1)]
+            return tuple(acc)
+
+        return one
+
+    def own_pairs(step):
+        return [(place, place - step - 1) for place in range(step + 1, groups)]
+
+    def edge_pairs(step):
+        return [(place, groups - 1 + place - step) for place in range(step + 1)]
+
+    own_late = jnp.transpose(lax.fori_loop(0, SUB, short_late, jnp.zeros((LANES, CHANNELS), f32)))
+    early = tuple(jnp.zeros((SUB, CHANNELS), f32) for _ in range(groups))
+    early = lax.fori_loop(0, SUB, short_early(LANES + SUB, own_pairs), early)
 
     loads[3].wait()
 
     edge.wait_recv()
     before = jnp.transpose(edge_ref[...].astype(f32))
-    border_ref[:LANES, :] = jnp.where(block_pos == 0, jnp.zeros_like(before), before)
-
-    pieces = [short_filter(border_ref, 64 * n, 64, 64 * n) for n in (0, 1)]
-    short_early = jnp.transpose(own_early + jnp.concatenate(pieces, axis=0))
-    gated = key_ref[...].astype(f32) * jnp.concatenate([short_early, own_late], axis=1)
+    window_ref[:LANES, :] = jnp.where(block_pos == 0, jnp.zeros_like(before), before)
+
+    early = lax.fori_loop(0, SUB, short_early(SUB, edge_pairs), early)
+    short_out = jnp.transpose(jnp.concatenate(early, axis=0))
+    gated = key_ref[...].astype(f32) * jnp.concatenate([short_out, own_late], axis=1)
     send_g[...] = to_sets(gated)
     to_outer(send_g, recv_g, 1)
 
@@ -332,7 +347,7 @@
     anywhere = pl.BlockSpec(memory_space=pl.ANY)
     return pl.pallas_call(
         functools.partial(kernel, sizes),
-        out_shape=jax.ShapeDtypeStruct((CHANNELS, LENGTH), bf16),
+        out_shape=pltpu.VMEM((CHANNELS, LENGTH), bf16),
         in_specs=[anywhere] * 6
         + [pl.BlockSpec(memory_space=pltpu.SMEM), pl.BlockSpec(memory_space=pltpu.VMEM)],
         out_specs=pl.BlockSpec(memory_space=pltpu.VMEM),
@@ -345,7 +360,6 @@
             pltpu.VMEM(lane_all.shape, bf16),
             pltpu.VMEM((CHANNELS, LANES), bf16),
             pltpu.VMEM((LANES + LENGTH, CHANNELS), f32),
-            pltpu.VMEM((2 * LANES, CHANNELS), f32),
             pltpu.VMEM((LANES, CHANNELS), f32),
             pltpu.VMEM((CHANNELS, LENGTH), f32),
             pltpu.VMEM((2, *fine), f32),

time: 56 us -> 54.7 us (0.977)
  local copies, waits for them, and re-layouts: 1.47 us -> 0.63 us
    unnamed x1, local copies, waits for them, and re-layouts: 1.47 us -> 0.63 us
where the time goes in v3:
time: 54.7 us; the launch traced here: 54.5 us
  Pallas kernels  53.9 us (99%)
  local copies, waits for them, and re-layouts  0.63 us (1%)
    pallas_call x1, Pallas kernels, shards(): pl.pallas_call(functools.partial(kernel, sizes), out_shape=pltpu.VMEM((CH...  53.9 us

profile of v3, /device:TPU:1, one launch (start us, length us, event | category | flops | bytes accessed | tf_op | source)
XLA Modules:
  0.0 54.5 jit_solution(5276620803926024723)
XLA Ops:
  0.0 53.9 %shard_map.82 = bf16[128,256]{1,0:T(8,128)(2,1)S(1)} custom-call(bf16[128,256]{1,0:T(8,128)(2,1)} %query_hbm.1, bf16[128,256]{1,0:T(8,128)(2,1)} %key_hbm.1, bf16[128,256]{1,0:T(8,128)(2,1)} %value_hbm.1, f32[128,128]{1,0:T(8,128)} %taps_hbm.1, f32[128,256]{1,0:T(8,128)} %filter_hbm.1, bf16[4,256,256]{2,1,0:T(8,128)(2,1)} %constant.2.clone.lane_hbm, ...), custom_call_target="tpu_custom_call" | custom-call | tf_op jit(solution)/shard_map/pallas_call | solution.py:348
  53.9 0.6 %copy.10 = bf16[128,256]{1,0:T(8,128)(2,1)} copy(bf16[128,256]{1,0:T(8,128)(2,1)S(1)} %shard_map.82) | data formatting | bytes 131072

commit v4 on v3

--- a/solution.py
+++ b/solution.py
@@ -107,9 +107,9 @@
 
 
 def kernel(
-    sizes, query_hbm, key_hbm, value_hbm, taps_hbm, filter_hbm, lane_hbm, counts_ref, skip_ref,
+    sizes, query_hbm, key_hbm, value_hbm, taps_hbm, filter_hbm, lane_hbm, counts_hbm, skip_hbm,
     out_ref,
-    query_ref, key_ref, value_ref, taps_ref, filter_ref, lane_ref,
+    query_ref, key_ref, value_ref, taps_ref, filter_ref, lane_ref, counts_ref, skip_ref,
     edge_ref, window_ref, kept_ref, skipped_ref, twist_ref, twiddle_ref, small_ref, spec_ref, start_ref,
     send_h, send_g, send_y, recv_h, recv_g, recv_y, mid_send, mid_recv,
     load_sem, far_send, far_recv, mid_send_sem, mid_recv_sem, edge_sem,
@@ -136,6 +136,7 @@
             [
                 (value_hbm, value_ref), (filter_hbm, filter_ref), (taps_hbm, taps_ref),
                 (key_hbm, key_ref), (query_hbm, query_ref), (lane_hbm, lane_ref),
+                (counts_hbm, counts_ref), (skip_hbm, skip_ref),
             ]
         )
     ]
@@ -192,6 +193,7 @@
     to_outer(send_h, recv_h, 0)
 
     loads[2].wait()
+    loads[6].wait()
     lane = iota((1, LANES), 1)
     counts = jnp.zeros((1, LANES), jnp.int32)
     first_group = lax.axis_index("chan") * (CHANNELS // GROUP_CH)
@@ -247,6 +249,7 @@
     send_g[...] = to_sets(gated)
     to_outer(send_g, recv_g, 1)
 
+    loads[7].wait()
     skip_eye = iota((CHANNELS, CHANNELS), 0) == iota((CHANNELS, CHANNELS), 1)
     skip_col = jnp.sum(jnp.where(skip_eye, skip_ref[...], 0.0), axis=1, keepdims=True)
     skipped_ref[...] = skip_col * gated
@@ -348,8 +351,7 @@
     return pl.pallas_call(
         functools.partial(kernel, sizes),
         out_shape=pltpu.VMEM((CHANNELS, LENGTH), bf16),
-        in_specs=[anywhere] * 6
-        + [pl.BlockSpec(memory_space=pltpu.SMEM), pl.BlockSpec(memory_space=pltpu.VMEM)],
+        in_specs=[anywhere] * 8,
         out_specs=pl.BlockSpec(memory_space=pltpu.VMEM),
         scratch_shapes=[
             pltpu.VMEM((CHANNELS, LENGTH), bf16),
@@ -358,6 +360,8 @@
             pltpu.VMEM((CHANNELS, LANES), f32),
             pltpu.VMEM((CHANNELS, LENGTH), f32),
             pltpu.VMEM(lane_all.shape, bf16),
+            pltpu.SMEM(tap_counts.shape, jnp.int32),
+            pltpu.VMEM((1, CHANNELS), f32),
             pltpu.VMEM((CHANNELS, LANES), bf16),
             pltpu.VMEM((LANES + LENGTH, CHANNELS), f32),
             pltpu.VMEM((LANES, CHANNELS), f32),
@@ -370,7 +374,7 @@
             *[pltpu.VMEM(sets, bf16)] * 6,
             pltpu.VMEM((3, inner_count, 4 * SUB, LANES), bf16),
             pltpu.VMEM((3, inner_count, 4 * SUB, LANES), bf16),
-            pltpu.SemaphoreType.DMA((6,)),
+            pltpu.SemaphoreType.DMA((8,)),
             pltpu.SemaphoreType.DMA((3,)),
             pltpu.SemaphoreType.DMA((3,)),
             pltpu.SemaphoreType.DMA((3,)),

time: 54.7 us -> 54 us (0.987)
  Pallas kernels: 53.9 us -> 53.2 us
    pallas_call x1, Pallas kernels: 53.9 us -> 53.2 us  [shards(): pl.pallas_call(functools.partial(kernel, sizes), out_shape=pltpu.VMEM((CH...]
where the time goes in v4:
time: 54 us; the launch traced here: 53.9 us
  Pallas kernels  53.2 us (99%)
  local copies, waits for them, and re-layouts  0.63 us (1%)
    pallas_call x1, Pallas kernels, shards(): pl.pallas_call(functools.partial(kernel, sizes), out_shape=pltpu.VMEM((CH...  53.2 us

profile of v4, /device:TPU:1, one launch (start us, length us, event | category | flops | bytes accessed | tf_op | source)
XLA Modules:
  0.0 53.9 jit_solution(13400581354961090207)
XLA Ops:
  0.0 53.2 %shard_map.82 = bf16[128,256]{1,0:T(8,128)(2,1)S(1)} custom-call(bf16[128,256]{1,0:T(8,128)(2,1)} %query_hbm.1, bf16[128,256]{1,0:T(8,128)(2,1)} %key_hbm.1, bf16[128,256]{1,0:T(8,128)(2,1)} %value_hbm.1, f32[128,128]{1,0:T(8,128)} %taps_hbm.1, f32[128,256]{1,0:T(8,128)} %filter_hbm.1, bf16[4,256,256]{2,1,0:T(8,128)(2,1)} %constant.2.clone.lane_hbm, ...), custom_call_target="tpu_custom_call" | custom-call | tf_op jit(solution)/shard_map/pallas_call | solution.py:351
  53.3 0.6 %copy.10 = bf16[128,256]{1,0:T(8,128)(2,1)} copy(bf16[128,256]{1,0:T(8,128)(2,1)S(1)} %shard_map.82) | data formatting | bytes 131072

commit v5 on v4

--- a/solution.py
+++ b/solution.py
@@ -110,7 +110,7 @@
     sizes, query_hbm, key_hbm, value_hbm, taps_hbm, filter_hbm, lane_hbm, counts_hbm, skip_hbm,
     out_ref,
     query_ref, key_ref, value_ref, taps_ref, filter_ref, lane_ref, counts_ref, skip_ref,
-    edge_ref, window_ref, kept_ref, skipped_ref, twist_ref, twiddle_ref, small_ref, spec_ref, start_ref,
+    edge_ref, border_ref, window_ref, kept_ref, skipped_ref, twist_ref, twiddle_ref, small_ref, spec_ref, start_ref,
     send_h, send_g, send_y, recv_h, recv_g, recv_y, mid_send, mid_recv,
     load_sem, far_send, far_recv, mid_send_sem, mid_recv_sem, edge_sem,
 ):
@@ -120,6 +120,7 @@
     fine = 2 * inner_count
     outer_pos, inner_pos = lax.axis_index("outer"), lax.axis_index("inner")
     block_pos = outer_pos * inner_count + inner_pos
+    side = 1 - 2 * lax.rem(inner_pos, 2)
 
     def block_id(pos):
         return {"outer": pos // inner_count, "inner": lax.rem(pos, inner_count)}
@@ -169,7 +170,7 @@
 
     def to_outer(send_ref, recv_ref, stream):
         for offset in order(outer_count):
-            target = lax.rem(outer_pos + offset, outer_count)
+            target = lax.rem(outer_pos + outer_count + side * offset, outer_count)
             pltpu.make_async_remote_copy(
                 src_ref=send_ref.at[target], dst_ref=recv_ref.at[outer_pos],
                 send_sem=far_send.at[stream], recv_sem=far_recv.at[stream],
@@ -181,10 +182,11 @@
     send_h[...] = to_sets(filter_ref[...])
     loads[0].wait()
     window_ref[LANES:, :] = jnp.transpose(value_ref[...].astype(f32))
+    border_ref[...] = window_ref[LENGTH:, :].astype(bf16)
 
     pl.semaphore_wait(barrier, outer_count + inner_count)
     edge = pltpu.make_async_remote_copy(
-        src_ref=value_ref.at[:, pl.ds(LANES, LANES)], dst_ref=edge_ref,
+        src_ref=border_ref, dst_ref=edge_ref,
         send_sem=edge_sem.at[0], recv_sem=edge_sem.at[1],
         device_id=following, device_id_type=MESH,
     )
@@ -240,7 +242,7 @@
     loads[3].wait()
 
     edge.wait_recv()
-    before = jnp.transpose(edge_ref[...].astype(f32))
+    before = edge_ref[...].astype(f32)
     window_ref[:LANES, :] = jnp.where(block_pos == 0, jnp.zeros_like(before), before)
 
     early = lax.fori_loop(0, SUB, short_early(SUB, edge_pairs), early)
@@ -275,7 +277,7 @@
 
     def exchange_inner(stream):
         for offset in order(inner_count):
-            peer = lax.rem(inner_pos + offset, inner_count)
+            peer = lax.rem(inner_pos + inner_count + side * offset, inner_count)
             pltpu.make_async_remote_copy(
                 src_ref=mid_send.at[stream, peer], dst_ref=mid_recv.at[stream, inner_pos],
                 send_sem=mid_send_sem.at[stream], recv_sem=mid_recv_sem.at[stream],
@@ -362,7 +364,8 @@
             pltpu.VMEM(lane_all.shape, bf16),
             pltpu.SMEM(tap_counts.shape, jnp.int32),
             pltpu.VMEM((1, CHANNELS), f32),
-            pltpu.VMEM((CHANNELS, LANES), bf16),
+            pltpu.VMEM((LANES, CHANNELS), bf16),
+            pltpu.VMEM((LANES, CHANNELS), bf16),
             pltpu.VMEM((LANES + LENGTH, CHANNELS), f32),
             pltpu.VMEM((LANES, CHANNELS), f32),
             pltpu.VMEM((CHANNELS, LENGTH), f32),

time: 54 us -> 54.2 us (level)
  no operation moved by 1% of the time
where the time goes in v5:
time: 54.2 us; the launch traced here: 53.9 us
  Pallas kernels  53.2 us (98%)
  local copies, waits for them, and re-layouts  0.63 us (1%)
    pallas_call x1, Pallas kernels, shards(): pl.pallas_call(functools.partial(kernel, sizes), out_shape=pltpu.VMEM((CH...  53.2 us

profile of v5, /device:TPU:1, one launch (start us, length us, event | category | flops | bytes accessed | tf_op | source)
XLA Modules:
  0.0 53.9 jit_solution(10471234947547779878)
XLA Ops:
  0.0 53.2 %shard_map.82 = bf16[128,256]{1,0:T(8,128)(2,1)S(1)} custom-call(bf16[128,256]{1,0:T(8,128)(2,1)} %query_hbm.1, bf16[128,256]{1,0:T(8,128)(2,1)} %key_hbm.1, bf16[128,256]{1,0:T(8,128)(2,1)} %value_hbm.1, f32[128,128]{1,0:T(8,128)} %taps_hbm.1, f32[128,256]{1,0:T(8,128)} %filter_hbm.1, bf16[4,256,256]{2,1,0:T(8,128)(2,1)} %constant.2.clone.lane_hbm, ...), custom_call_target="tpu_custom_call" | custom-call | tf_op jit(solution)/shard_map/pallas_call | solution.py:353
  53.2 0.6 %copy.10 = bf16[128,256]{1,0:T(8,128)(2,1)} copy(bf16[128,256]{1,0:T(8,128)(2,1)S(1)} %shard_map.82) | data formatting | bytes 131072
